TPU v7x, 32 devices: a whole 2x2x4 slice. The times are simulated.
32 devices in a mesh: pairs: 8 (over z, x), hours: 4 (over y, core).
Axes of the slice: x: 2, y: 2, z: 4, core: 2. Of those that a mesh axis runs over, the one named last changes fastest.
Arguments:
- records: bfloat16 [1024, 4, 3600], P('pairs', 'hours'), may hold values from -100 to 100
- usable: int32 [1024, 4], P('pairs', 'hours'), may hold values from 0 to 1, as said below
- pair_blocks: int32 [8, 2], P('pairs'), may hold values from 0 to 7
Outputs:
- correlations: float32 [8, 128, 128, 256], P('pairs', 'hours')
Inputs may be any that keep to these rules, and one draw needn't show every extreme that they name: Some stations are usable in no hour at all. `pair_blocks`: each row names two station blocks; a block may appear in many rows and both entries may be equal.
All inputs are finite; a program needn't handle non-finite values.
Results may differ from a plain program's by a relative error of at most 0.0071.
Values may be sent and summed in bfloat16 or wider, within the bound.
A program may use at most 128 MiB of HBM per device.

v0:
```python
import math

import jax
import jax.numpy as jnp
from jax import lax
from jax.sharding import PartitionSpec as P

L = 3600
F = 512
W = 32
F0 = 64
LAGS = 256


def spectrum_table():
    extent = F + 2 * W
    freq_bins = F0 - W + jnp.arange(extent, dtype=jnp.int32)
    samples = jnp.arange(L, dtype=jnp.int32)
    phases = samples[:, None] * freq_bins[None, :] % L
    angles = 2.0 * math.pi / L * phases.astype(jnp.float32)
    factor = 1.0 / math.sqrt(L)
    return jnp.concatenate([jnp.cos(angles) * factor, -jnp.sin(angles) * factor], axis=1).astype(
        jnp.bfloat16
    )


def smoothing_matrix():
    extent = F + 2 * W
    source = jnp.arange(extent, dtype=jnp.int32)[:, None]
    target = jnp.arange(F, dtype=jnp.int32)[None, :]
    spacing = source - target
    within = (spacing >= 0) & (spacing <= 2 * W)
    return jnp.where(within, jnp.float32(1.0 / (2 * W + 1)), jnp.float32(0.0))


def lag_weights():
    freq_bins = F0 + jnp.arange(F, dtype=jnp.int32)
    shifts = jnp.arange(LAGS, dtype=jnp.int32) - LAGS // 2
    phases = freq_bins[:, None] * shifts[None, :] % L
    angles = 2.0 * math.pi / L * phases.astype(jnp.float32)
    factor = 1.0 / math.sqrt(F)
    return jnp.concatenate([jnp.cos(angles) * factor, -jnp.sin(angles) * factor], axis=0).astype(
        jnp.bfloat16
    )


def whiten(signal, usable_flags):
    station_rows, hour_count = (signal.shape[0], signal.shape[1])
    flat = signal.reshape(station_rows * hour_count, L)
    spectra = jnp.dot(flat, spectrum_table(), preferred_element_type=jnp.float32)
    extent = F + 2 * W
    real_part = spectra[:, :extent]
    imag_part = spectra[:, extent:]
    power = real_part * real_part + imag_part * imag_part
    smooth = jnp.dot(power, smoothing_matrix(), precision=lax.Precision.HIGHEST)
    weight = usable_flags.astype(jnp.float32) / jnp.sqrt(smooth + 1e-05)
    whitened = jnp.concatenate(
        [real_part[:, W : W + F] * weight, imag_part[:, W : W + F] * weight], axis=1
    )
    return whitened.astype(jnp.bfloat16).reshape(station_rows, hour_count, 2 * F)


def hour_cross(first_hour, second_hour):
    first_real = first_hour[:, :F].astype(jnp.float32)
    first_imag = first_hour[:, F:].astype(jnp.float32)
    second_real = second_hour[:, :F].astype(jnp.float32)
    second_imag = second_hour[:, F:].astype(jnp.float32)
    cross_real = (
        first_real[:, None, :] * second_real[None, :, :]
        + first_imag[:, None, :] * second_imag[None, :, :]
    )
    cross_imag = (
        first_imag[:, None, :] * second_real[None, :, :]
        - first_real[:, None, :] * second_imag[None, :, :]
    )
    return jnp.concatenate([cross_real, cross_imag], axis=2).astype(jnp.bfloat16)


def correlate(first_block, second_block, first_flags, second_flags, weights):
    first_rows = first_block.shape[0]
    second_rows = second_block.shape[0]

    def add_hour(hour_step, running):
        first_hour = lax.dynamic_index_in_dim(first_block, hour_step, 1, keepdims=False)
        second_hour = lax.dynamic_index_in_dim(second_block, hour_step, 1, keepdims=False)
        cross = hour_cross(first_hour, second_hour)
        lagged = jnp.dot(
            cross.reshape(first_rows * second_rows, 2 * F),
            weights,
            preferred_element_type=jnp.float32,
        )
        return running + lagged.reshape(first_rows, second_rows, LAGS)

    stacks = lax.fori_loop(
        0, first_block.shape[1], add_hour, jnp.zeros((first_rows, second_rows, LAGS), jnp.float32)
    )
    counts = jnp.dot(
        first_flags.astype(jnp.float32),
        second_flags.astype(jnp.float32).T,
        precision=lax.Precision.HIGHEST,
    )
    return (stacks, counts)


def correlate_tiles(first_side, second_side, first_marks, second_marks, weights):
    stacks, counts = correlate(
        first_side[0], second_side[0], first_marks[0], second_marks[0], weights
    )
    stack_list = [stacks]
    count_list = [counts]
    return (jnp.stack(stack_list), jnp.stack(count_list))


def body(records, usable, pair_blocks):
    tiles = pair_blocks.shape[0]
    wanted = pair_blocks.reshape(-1)
    block_rows = records.shape[0]
    hour_count = records.shape[1]
    weights = lag_weights()
    usable_marks = usable.astype(jnp.bfloat16)
    empty_marks = jnp.zeros((2 * tiles, block_rows, hour_count), jnp.bfloat16)
    initial = (jnp.zeros((2 * tiles, block_rows, hour_count, L), jnp.bfloat16), empty_marks)
    pieces_in = (
        lax.all_gather(records, "pairs", axis=0, tiled=True),
        lax.all_gather(usable_marks, "pairs", axis=0, tiled=True),
    )
    piece_rows = pieces_in[0].shape[0]
    block_count = piece_rows // block_rows
    block_ids = jnp.arange(block_count, dtype=jnp.int32)
    matches = wanted[:, None] == block_ids[None, :]
    hit = jnp.any(matches, axis=1)
    selector = matches.astype(jnp.bfloat16)
    picked = jnp.dot(
        selector, pieces_in[0].reshape(block_count, -1), preferred_element_type=jnp.float32
    )
    picked = picked.astype(jnp.bfloat16).reshape(initial[0].shape)
    picked_marks = jnp.dot(
        selector, pieces_in[1].reshape(block_count, -1), preferred_element_type=jnp.float32
    )
    picked_marks = picked_marks.astype(jnp.bfloat16).reshape(initial[1].shape)
    raw_slots = jnp.where(hit[:, None, None, None], picked, initial[0])
    slot_marks = jnp.where(hit[:, None, None], picked_marks, initial[1])
    slots = whiten(
        raw_slots.reshape(2 * tiles * block_rows, hour_count, L),
        slot_marks.reshape(2 * tiles * block_rows, hour_count),
    )
    slots = slots.reshape(2 * tiles, block_rows, hour_count, 2 * F)
    paired = slots.reshape(tiles, 2, block_rows, hour_count, 2 * F)
    paired_marks = slot_marks.reshape(tiles, 2, block_rows, hour_count)
    first_side = paired[:, 0]
    second_side = paired[:, 1]
    first_marks = paired_marks[:, 0]
    second_marks = paired_marks[:, 1]
    first_rows, first_rows_marks = (
        lax.all_to_all(first_side, "hours", split_axis=1, concat_axis=2, tiled=True),
        lax.all_to_all(first_marks, "hours", split_axis=1, concat_axis=2, tiled=True),
    )
    second_all, second_all_marks = (
        lax.all_gather(second_side, "hours", axis=2, tiled=True),
        lax.all_gather(second_marks, "hours", axis=2, tiled=True),
    )
    stacks, counts = correlate_tiles(
        first_rows, second_all, first_rows_marks, second_all_marks, weights
    )
    return stacks / jnp.maximum(counts, 1.0)[..., None]


def solution(mesh):
    return jax.shard_map(
        body,
        mesh=mesh,
        in_specs=(P("pairs", "hours", None), P("pairs", "hours"), P("pairs", None)),
        out_specs=P("pairs", "hours", None, None),
        check_vma=False,
    )
```

profile of v0, /device:TPU:1, one launch (start us, length us, event | category | flops | bytes accessed | tf_op | source)
XLA Modules:
  0.0 272.8 jit_solution(4675151594216595915)
XLA Ops:
  6.5 0.7 all-gather.5.cloned.1.call-update
  7.3 0.7 convert_element_type.80
  8.0 17.9 %all_gather.13 = bf16[1024,1]{0,1:T(2,128)(2,1)S(1)} all-gather(bf16[128,1]{0,1:T(2,128)(2,1)S(1)} %convert_element_type.80), channel_id=1, replica_groups=mesh['pairs'=8,'hours'=4] {'pairs'}, dimensions={0}, use_global_device_ids=true | all-gather | bytes 2304 | tf_op jit(solution)/shard_map/all_gather | solution.py:125
  25.9 0.8 fusion.49
  26.8 0.1 broadcast_bitcast_fusion
  26.9 0.8 bitcast_convert_fusion
  27.7 40.2 %multiply_convert_fusion.1 = (bf16[3600,576]{1,0:T(8,128)(2,1)}, bf16[3600,576]{1,0:T(8,128)(2,1)}) fusion(s32[576]{0:T(1024)S(1)} %iota_add_fusion), kind=kLoop, calls=%fused_computation.20 | loop fusion | flops 29030400 | bytes 8296704 | tf_op jit(solution)/shard_map/convert.9
  67.9 55.3 %all-gather.5.cloned.1.call-done = bf16[1024,1,3600]{0,2,1:T(8,128)(2,1)} async-done(((bf16[128,1,3600]{0,2,1:T(8,128)(2,1)}), bf16[1024,1,3600]{0,2,1:T(8,128)(2,1)}) %all-gather.5.cloned.1.call-update) | async-done | bytes 7372816 | tf_op jit(solution)/shard_map/all_gather | solution.py:124
  123.3 10.1 %copy.22 = bf16[1024,1,3600]{2,0,1:T(8,128)(2,1)} copy(bf16[1024,1,3600]{0,2,1:T(8,128)(2,1)} %all-gather.5.cloned.1.call-done) | data formatting | bytes 14745600 | tf_op jit(solution)/shard_map/all_gather | solution.py:124
  133.3 12.8 %reshape.118 = bf16[3686400]{0:T(1024)(128)(2,1)} reshape(bf16[1,1024,3600]{2,1,0:T(8,128)(2,1)} %bitcast.62) | data formatting | bytes 14745600
  146.1 9.1 %reshape.106 = bf16[8,460800]{1,0:T(8,128)(2,1)} reshape(bf16[3686400]{0:T(1024)(128)(2,1)} %reshape.118) | data formatting | bytes 14745600 | tf_op jit(solution)/shard_map/reshape | solution.py:134
  155.2 5.2 %convolution_convert_fusion = bf16[2,460800]{1,0:T(2,128)(2,1)S(1)} fusion(bf16[8,460800]{1,0:T(8,128)(2,1)} %reshape.106, s32[2]{0:T(128)S(1)} %bitcast.72), kind=kOutput, calls=%fused_computation.15 | convolution fusion | flops 15667216 | bytes 9216008 | tf_op jit(solution)/shard_map/dot_general | solution.py:133
  160.5 2.4 reshape.120
  162.8 3.9 %reshape.107 = bf16[256,3600]{1,0:T(8,128)(2,1)S(1)} reshape(bf16[921600]{0:T(1024)(128)(2,1)} %reshape.120) | data formatting | bytes 3686400 | tf_op jit(solution)/shard_map/reshape | solution.py:136
  166.8 6.6 %fusion.13 = f32[256,1152]{1,0:T(8,128)S(1)} fusion(bf16[3600,576]{1,0:T(8,128)(2,1)} %get-tuple-element.139, bf16[3600,576]{1,0:T(8,128)(2,1)} %get-tuple-element.138, bf16[256,3600]{1,0:T(8,128)(2,1)S(1)} %reshape.107, pred[256]{0:T(512)(128)(4,1)S(1)} %broadcast_bitcast_fusion), kind=kOutput, calls=%fused_computation.25 | convolution fusion | flops 2140876800 | bytes 11317504 | tf_op jit(solution)/shard_map/dot_general | solution.py:50
  173.4 1.5 fusion.37
  174.9 0.8 fusion.44
  175.7 0.8 copy.27
  176.5 4.7 %all-to-all-start.1 = ((bf16[1,128,1]{2,0,1:T(2,128)(2,1)}), bf16[1,128,1]{2,0,1:T(2,128)(2,1)S(1)}, u32[]{:S(2)}, u32[]{:S(2)}) async-start(bf16[1,128,1]{2,0,1:T(2,128)(2,1)} %copy.27), calls=%async_computation.1 | async-start | bytes 131072 | tf_op jit(solution)/shard_map/all_to_all | solution.py:156
  181.2 5.1 %all-gather.1 = bf16[1,1,128,4]{2,1,0,3:T(2,128)(2,1)S(1)} all-gather(bf16[1,1,128,1]{2,1,0,3:T(2,128)(2,1)S(1)} %get-tuple-element.143), channel_id=3, replica_groups=mesh['pairs'=8,'hours'=4] {'hours'}, dimensions={3}, use_global_device_ids=true | all-gather | bytes 1280 | tf_op jit(solution)/shard_map/all_gather | solution.py:160
  186.3 2.6 multiply_convert_fusion.3
  188.9 1.0 reduce.1
  189.9 0.1 all_to_all.26
  190.0 0.4 copy.36
  190.4 0.6 broadcast.62
  191.0 2.2 reduce.2
  193.2 0.9 reshape.122
  194.1 3.6 %all-to-all-start = ((bf16[4,2,16384]{2,1,0:T(2,128)(2,1)}), bf16[4,2,16384]{2,1,0:T(2,128)(2,1)S(1)}, u32[]{:S(2)}, u32[]{:S(2)}) async-start(bf16[4,2,16384]{2,1,0:T(2,128)(2,1)} %reshape.122), calls=%async_computation | async-start | bytes 524288 | tf_op jit(solution)/shard_map/all_to_all | solution.py:155
  197.7 0.2 convolution_maximum_fusion
  197.9 5.4 %all-to-all-done = bf16[4,2,16384]{2,1,0:T(2,128)(2,1)S(1)} async-done(((bf16[4,2,16384]{2,1,0:T(2,128)(2,1)}), bf16[4,2,16384]{2,1,0:T(2,128)(2,1)S(1)}, u32[]{:S(2)}, u32[]{:S(2)}) %all-to-all-start) | async-done | bytes 262176 | tf_op jit(solution)/shard_map/all_to_all | solution.py:155
  203.3 0.3 reshape.123
  203.6 0.1 copy.29
  203.7 58.3 %while.14 = (s32[]{:T(128)}, f32[32,128,256]{2,1,0:T(8,128)}, bf16[32,4,1024]{2,0,1:T(8,128)(2,1)S(1)}, bf16[128,4,1024]{2,0,1:T(8,128)(2,1)}, bf16[1024,256]{1,0:T(8,128)(2,1)S(1)}, /*index=5*/s32[]{:T(128)}, s32[]{:T(128)}) while((s32[]{:T(128)}, f32[32,128,256]{2,1,0:T(8,128)}, bf16[32,4,1024]{2,0,1:T(8,128)(2,1)S(1)}, ...), condition=%wide.region_2.3_spmd.clone, body=%wide.region_1.2_spmd.clone.sunk | while | flops 2183299072 | bytes 27983964 | solution.py:94
  203.7 1.0 dynamic-slice_bitcast_fusion.4
  204.7 0.1 slice_convert_fusion.6
  204.8 4.8 %add_convert_fusion.2 = (bf16[32,128,512]{2,1,0:T(8,128)(2,1)}, bf16[32,128,512]{2,1,0:T(8,128)(2,1)}) fusion(f32[128,512]{1,0:T(8,128)S(1)} %get-tuple-element.183, f32[32,512]{1,0:T(8,128)S(1)} %get-tuple-element.184, f32[128,512]{1,0:T(8,128)S(1)} %get-tuple-element.185, f32[32,512]{1,0:T(8,128)S(1)} %get-tuple-element.186), kind=kLoop, calls=%fused_computation.5.clone.1 | loop fusion | flops 16777216 | bytes 9043968 | tf_op jit(solution)/shard_map/convert
  209.6 7.8 %select_add_fusion.2 = f32[32,128,256]{2,1,0:T(8,128)} fusion(f32[32,128,256]{2,1,0:T(8,128)} %get-tuple-element.197, pred[]{:T(512)S(6)} %compare.3, bf16[32,128,512]{2,1,0:T(8,128)(2,1)} %get-tuple-element.187, bf16[32,128,512]{2,1,0:T(8,128)(2,1)} %get-tuple-element.188, bf16[1024,256]{1,0:T(8,128)(2,1)S(1)} %get-tuple-element.207), kind=kOutput, calls=%fused_computation.6.clone.1 | convolution fusion | flops 2166358016 | bytes 17301504 | tf_op jit(solution)/shard_map/while/body/eval_jaxpr/dot_general | solution.py:87
  217.4 1.0 dynamic-slice_bitcast_fusion.4
  218.4 0.1 slice_convert_fusion.6
  218.5 4.8 %add_convert_fusion.2 = (bf16[32,128,512]{2,1,0:T(8,128)(2,1)}, bf16[32,128,512]{2,1,0:T(8,128)(2,1)}) fusion(f32[128,512]{1,0:T(8,128)S(1)} %get-tuple-element.183, f32[32,512]{1,0:T(8,128)S(1)} %get-tuple-element.184, f32[128,512]{1,0:T(8,128)S(1)} %get-tuple-element.185, f32[32,512]{1,0:T(8,128)S(1)} %get-tuple-element.186), kind=kLoop, calls=%fused_computation.5.clone.1 | loop fusion | flops 16777216 | bytes 9043968 | tf_op jit(solution)/shard_map/convert
  223.2 9.0 %select_add_fusion.2 = f32[32,128,256]{2,1,0:T(8,128)} fusion(f32[32,128,256]{2,1,0:T(8,128)} %get-tuple-element.197, pred[]{:T(512)S(6)} %compare.3, bf16[32,128,512]{2,1,0:T(8,128)(2,1)} %get-tuple-element.187, bf16[32,128,512]{2,1,0:T(8,128)(2,1)} %get-tuple-element.188, bf16[1024,256]{1,0:T(8,128)(2,1)S(1)} %get-tuple-element.207), kind=kOutput, calls=%fused_computation.6.clone.1 | convolution fusion | flops 2166358016 | bytes 17301504 | tf_op jit(solution)/shard_map/while/body/eval_jaxpr/dot_general | solution.py:87
  232.3 1.0 dynamic-slice_bitcast_fusion.4
  233.3 4.8 %add_convert_fusion.2 = (bf16[32,128,512]{2,1,0:T(8,128)(2,1)}, bf16[32,128,512]{2,1,0:T(8,128)(2,1)}) fusion(f32[128,512]{1,0:T(8,128)S(1)} %get-tuple-element.183, f32[32,512]{1,0:T(8,128)S(1)} %get-tuple-element.184, f32[128,512]{1,0:T(8,128)S(1)} %get-tuple-element.185, f32[32,512]{1,0:T(8,128)S(1)} %get-tuple-element.186), kind=kLoop, calls=%fused_computation.5.clone.1 | loop fusion | flops 16777216 | bytes 9043968 | tf_op jit(solution)/shard_map/convert
  238.1 9.0 %select_add_fusion.2 = f32[32,128,256]{2,1,0:T(8,128)} fusion(f32[32,128,256]{2,1,0:T(8,128)} %get-tuple-element.197, pred[]{:T(512)S(6)} %compare.3, bf16[32,128,512]{2,1,0:T(8,128)(2,1)} %get-tuple-element.187, bf16[32,128,512]{2,1,0:T(8,128)(2,1)} %get-tuple-element.188, bf16[1024,256]{1,0:T(8,128)(2,1)S(1)} %get-tuple-element.207), kind=kOutput, calls=%fused_computation.6.clone.1 | convolution fusion | flops 2166358016 | bytes 17301504 | tf_op jit(solution)/shard_map/while/body/eval_jaxpr/dot_general | solution.py:87
  247.1 1.0 dynamic-slice_bitcast_fusion.4
  248.2 4.8 %add_convert_fusion.2 = (bf16[32,128,512]{2,1,0:T(8,128)(2,1)}, bf16[32,128,512]{2,1,0:T(8,128)(2,1)}) fusion(f32[128,512]{1,0:T(8,128)S(1)} %get-tuple-element.183, f32[32,512]{1,0:T(8,128)S(1)} %get-tuple-element.184, f32[128,512]{1,0:T(8,128)S(1)} %get-tuple-element.185, f32[32,512]{1,0:T(8,128)S(1)} %get-tuple-element.186), kind=kLoop, calls=%fused_computation.5.clone.1 | loop fusion | flops 16777216 | bytes 9043968 | tf_op jit(solution)/shard_map/convert
  253.0 9.0 %select_add_fusion.2 = f32[32,128,256]{2,1,0:T(8,128)} fusion(f32[32,128,256]{2,1,0:T(8,128)} %get-tuple-element.197, pred[]{:T(512)S(6)} %compare.3, bf16[32,128,512]{2,1,0:T(8,128)(2,1)} %get-tuple-element.187, bf16[32,128,512]{2,1,0:T(8,128)(2,1)} %get-tuple-element.188, bf16[1024,256]{1,0:T(8,128)(2,1)S(1)} %get-tuple-element.207), kind=kOutput, calls=%fused_computation.6.clone.1 | convolution fusion | flops 2166358016 | bytes 17301504 | tf_op jit(solution)/shard_map/while/body/eval_jaxpr/dot_general | solution.py:87
  262.0 3.9 %divide_bitcast_fusion = f32[1,32,128,256]{3,2,1,0:T(8,128)} fusion(f32[32,128,256]{2,1,0:T(8,128)} %get-tuple-element.99, f32[32,128]{1,0:T(8,128)S(1)} %convolution_maximum_fusion), kind=kLoop, calls=%fused_computation.29 | loop fusion | flops 1048576 | bytes 8404992 | tf_op jit(solution)/shard_map/div | solution.py:165
  (24 shorter events, 0.4 us)
Async XLA Ops:
  6.5 116.7 %all-gather.5.cloned.1.call-start = ((), (), s32[]{:S(2)}) async-start(), calls=%async_computation.2 | async-start | bytes 8294400 | tf_op jit(solution)/shard_map/all_gather | solution.py:124
  7.3 196.4 %all-gather.7.cloned.1.call-start = ((), (), s32[]{:S(2)}) async-start(), calls=%async_computation.3 | async-start | bytes 1310720 | tf_op jit(solution)/shard_map/all_gather | solution.py:159
  146.1 9.2 %copy-start = (s32[1,2]{1,0:T(1,128)S(1)}, s32[1,2]{1,0:T(1,128)}, u32[]{:S(2)}) copy-start(s32[1,2]{1,0:T(1,128)} %param.7) | copy-start | bytes 28
  176.5 12.4 %all-to-all-start.1 = ((bf16[1,128,1]{2,0,1:T(2,128)(2,1)}), bf16[1,128,1]{2,0,1:T(2,128)(2,1)S(1)}, u32[]{:S(2)}, u32[]{:S(2)}) async-start(bf16[1,128,1]{2,0,1:T(2,128)(2,1)} %copy.27), calls=%async_computation.1 | async-start | bytes 131072 | tf_op jit(solution)/shard_map/all_to_all | solution.py:156
  194.1 9.2 %all-to-all-start = ((bf16[4,2,16384]{2,1,0:T(2,128)(2,1)}), bf16[4,2,16384]{2,1,0:T(2,128)(2,1)S(1)}, u32[]{:S(2)}, u32[]{:S(2)}) async-start(bf16[4,2,16384]{2,1,0:T(2,128)(2,1)} %reshape.122), calls=%async_computation | async-start | bytes 524288 | tf_op jit(solution)/shard_map/all_to_all | solution.py:155
Sparse Core Ops, SparseCore 0:
  9.4 113.8 all-gather.4
  175.8 16.2 all-gather.6
where the time goes:
time: 275 us; the launch traced here: 273 us
  other arithmetic  71.7 us (26%)
  waiting for transfers between devices  61.4 us (22%)
  matrix products  49.3 us (18%)
  local copies, waits for them, and re-layouts  45.4 us (17%)
  blocking collectives  23 us (8%)
  between operations  13.5 us (5%)
  starting transfers between devices  8.36 us (3%)
    another operation x6, other arithmetic  61.9 us
    all_gather x1, waiting for transfers between devices, body(): lax.all_gather(records, 'pairs', axis=0, tiled=True)  55.3 us
    dot_general x4, matrix products, add_hour(): jnp.dot(cross.reshape(first_rows * second_rows, 2 * F), weights, preferre...  34.9 us
    all_gather x1, blocking collectives, body(): lax.all_gather(usable_marks, 'pairs', axis=0, tiled=True)  17.9 us
    unnamed x8, local copies, waits for them, and re-layouts  17 us
    all_gather x1, local copies, waits for them, and re-layouts, body(): lax.all_gather(records, 'pairs', axis=0, tiled=True)  10.1 us
    reshape x1, local copies, waits for them, and re-layouts, body(): pieces_in[0].reshape(block_count, -1)  9.15 us
    dot_general x1, matrix products, whiten(): jnp.dot(flat, spectrum_table(), preferred_element_type=jnp.float32)  6.58 us
  transfers between devices with their start and end apart: 4, of which 2 were waited for; matrix products, arithmetic and copies ran while one was open for 19% of the time, Pallas kernels for 0%

commit v1 on v0

v1 whole, which is shorter than its diff:
```python
import functools
import math

import jax
import jax.numpy as jnp
import numpy as np
from jax import lax
from jax.experimental import pallas as pl
from jax.experimental.pallas import tpu as pltpu
from jax.sharding import PartitionSpec as P

L = 3600
F = 512
W = 32
F0 = 64
LAGS = 256
EXTENT = F + 2 * W
HALF = L // 2
HE = EXTENT // 2
HF = F // 2
CORES = 2
MESH = pl.DeviceIdType.MESH


def cos_sin(phases, length, scale):
    angles = np.float32(2.0 * math.pi / length) * (phases % length).astype(np.float32)
    wide = angles.astype(np.float64)
    scale = np.float32(scale)
    return np.cos(wide).astype(np.float32) * scale, -np.sin(wide).astype(np.float32) * scale


def spectrum_tables():
    bins = F0 - W + np.arange(EXTENT)
    c, q = cos_sin(np.arange(HALF)[:, None] * bins[None, :], L, 1.0 / math.sqrt(L))
    even = np.concatenate([c[:, 0::2], q[:, 0::2]], axis=1)
    odd = np.concatenate([c[:, 1::2], q[:, 1::2]], axis=1)
    return even.astype(jnp.bfloat16), odd.astype(jnp.bfloat16)


def window_ones():
    source = np.concatenate([np.arange(0, EXTENT, 2), np.arange(1, EXTENT, 2)])
    target = np.concatenate([np.arange(0, F, 2), np.arange(1, F, 2)])
    gap = source[:, None] - target[None, :]
    return ((gap >= 0) & (gap <= 2 * W)).astype(np.float32).astype(jnp.bfloat16)


def lag_weights():
    order = np.concatenate([np.arange(0, F, 2), np.arange(1, F, 2)])
    shifts = np.arange(LAGS) - LAGS // 2
    c, s = cos_sin((F0 + order)[:, None] * shifts[None, :], L, 1.0 / math.sqrt(F))
    return np.concatenate([c, s], axis=0).astype(jnp.bfloat16)


def split_hi_lo(value):
    high = value.astype(jnp.bfloat16)
    low = (value - high.astype(jnp.float32)).astype(jnp.bfloat16)
    return jnp.concatenate([high, low], axis=0)


def whiten_kernel(u_ref, v_ref, flag_ref, even_ref, odd_ref, ones_ref, out_ref):
    rows = out_ref.shape[0]

    def transform(x_ref, table_ref):
        both = jnp.dot(x_ref[...], table_ref[...], preferred_element_type=jnp.float32)
        both = both[:rows] + both[rows:]
        return both[:, :HE], both[:, HE:]

    re_even, im_even = transform(u_ref, even_ref)
    re_odd, im_odd = transform(v_ref, odd_ref)
    power = jnp.concatenate(
        [re_even * re_even + im_even * im_even, re_odd * re_odd + im_odd * im_odd], axis=1
    )
    total = jnp.dot(split_hi_lo(power), ones_ref[...], preferred_element_type=jnp.float32)
    smooth = (total[:rows] + total[rows:]) * jnp.float32(1.0 / (2 * W + 1))
    weight = flag_ref[...] / jnp.sqrt(smooth + 1e-05)
    w2 = W // 2
    out_ref[:, 0:HF] = (re_even[:, w2 : w2 + HF] * weight[:, :HF]).astype(jnp.bfloat16)
    out_ref[:, HF:F] = (re_odd[:, w2 : w2 + HF] * weight[:, HF:]).astype(jnp.bfloat16)
    out_ref[:, F : F + HF] = (im_even[:, w2 : w2 + HF] * weight[:, :HF]).astype(jnp.bfloat16)
    out_ref[:, F + HF :] = (im_odd[:, w2 : w2 + HF] * weight[:, HF:]).astype(jnp.bfloat16)


def exchange_kernel(
    pairs, width, hours, pair_ref, w_ref, f_ref, bj, bi, bf,
    *scratch,
):
    g = scratch[:hours]
    (
        gf, sj, si, sf, zx_send, zx_recv, j_send, j_recv, relay_send, i_send, i_recv,
        f_send, f_recv, local_sem, keep_sem,
    ) = scratch[hours:]
    depth = pairs // width
    rows = w_ref.shape[0]
    part = rows // hours
    p = lax.axis_index("pairs")
    me = lax.axis_index("hours")
    z, x = p // width, p % width
    y, core = me // CORES, me % CORES
    partner = y * CORES + (1 - core)
    flags_unit = hours

    steps = (
        (z + 1 < depth, p + width),
        (z > 0, p - width),
        (x + 1 < width, p + 1),
        (x > 0, p - 1),
    )

    barrier = pltpu.get_barrier_semaphore()
    for exists, target in steps:
        @pl.when(exists)
        def _(target=target):
            pl.semaphore_signal(barrier, inc=1, device_id={"pairs": target}, device_id_type=MESH)
    for k in range(1, hours):
        pl.semaphore_signal(
            barrier, inc=1, device_id={"hours": (me + k) % hours}, device_id_type=MESH
        )
    near = sum(e.astype(jnp.int32) for e, _ in steps)
    pl.semaphore_wait(barrier, near + hours - 1)

    pending = []

    def slot(b, u):
        return gf.at[b] if u == flags_unit else g[u].at[b]

    def own(u):
        return f_ref if u == flags_unit else w_ref.at[pl.ds(u * part, part)]

    def forward(cond, b, u, way, is_own=False):
        exists, target = steps[way]
        both = exists if cond is None else jnp.logical_and(cond, exists)

        def make():
            return pltpu.make_async_remote_copy(
                src_ref=own(u) if is_own else slot(b, u),
                dst_ref=slot(b, u),
                send_sem=zx_send.at[way, b, u],
                recv_sem=zx_recv.at[b, u],
                device_id={"pairs": target},
                device_id_type=MESH,
            )

        @pl.when(both)
        def _():
            make().start()
        pending.append((both, make))

    def arrived(b, u):
        pltpu.make_async_remote_copy(
            src_ref=slot(b, u), dst_ref=slot(b, u), send_sem=zx_send.at[0, b, u],
            recv_sem=zx_recv.at[b, u], device_id={"pairs": p}, device_id_type=MESH,
        ).wait_recv()

    def send_own(u):
        for way in range(4):
            forward(None, p, u, way, is_own=True)

    keep = [
        pltpu.make_async_copy(own(u), slot(p, u), keep_sem.at[u]) for u in range(hours + 1)
    ]
    for copy in keep:
        copy.start()

    def gather(u):
        for d in range(1, depth):
            for way, b, cond in (
                (0, p - d * width, z - d >= 0),
                (1, p + d * width, z + d < depth),
            ):
                @pl.when(cond)
                def _(b=b):
                    arrived(b, u)
                for out in (way, 2, 3):
                    forward(cond, b, u, out)
        for d in range(1, width):
            for zz in range(depth):
                for way, b, cond in (
                    (2, zz * width + x - d, x - d >= 0),
                    (3, zz * width + x + d, x + d < width),
                ):
                    @pl.when(cond)
                    def _(b=b):
                        arrived(b, u)
                    if width > 2:
                        forward(cond, b, u, way)

    late = []

    def remote(src, dst, send_sem, recv_sem, target):
        copy = pltpu.make_async_remote_copy(
            src_ref=src, dst_ref=dst, send_sem=send_sem, recv_sem=recv_sem,
            device_id={"hours": target}, device_id_type=MESH,
        )
        copy.start()
        late.append(copy)

    def share(u):
        span = pl.ds(u * part, part)
        keep[u].wait()
        sj[u] = g[u][pair_ref[0, 1]]
        si[u] = g[u][pair_ref[0, 0]]
        for k in range(1, hours // CORES):
            target = ((y + k) % (hours // CORES)) * CORES + core
            remote(sj.at[u], bj.at[me, span], j_send.at[k, u], j_recv.at[me, u], target)
        remote(sj.at[u], bj.at[me, span], j_send.at[0, u], j_recv.at[me, u], partner)
        to_other = me != u

        def make():
            return pltpu.make_async_remote_copy(
                src_ref=si.at[u], dst_ref=bi.at[me], send_sem=i_send.at[u],
                recv_sem=i_recv.at[me], device_id={"hours": u}, device_id_type=MESH,
            )

        @pl.when(to_other)
        def _():
            make().start()
        pending.append((to_other, make))

        @pl.when(me == u)
        def _():
            pltpu.make_async_copy(si.at[u], bi.at[me], local_sem.at[2]).start()
        pltpu.make_async_copy(sj.at[u], bj.at[me, span], local_sem.at[3 + u]).start()

    def got(sem, ref):
        pltpu.make_async_remote_copy(
            src_ref=ref, dst_ref=ref, send_sem=sem, recv_sem=sem,
            device_id={"hours": me}, device_id_type=MESH,
        ).wait_recv()

    def relay(u):
        span = pl.ds(u * part, part)
        for k in range(1, hours // CORES):
            peer = ((y + k) % (hours // CORES)) * CORES + core
            got(j_recv.at[peer, u], bj.at[peer, span])
            remote(
                bj.at[peer, span], bj.at[peer, span], relay_send.at[k, u],
                j_recv.at[peer, u], partner,
            )

    send_own(flags_unit)
    send_own(0)
    for u in range(hours):
        if u + 1 < hours:
            send_own(u + 1)
        if u == 0:
            gather(flags_unit)
        gather(u)
        if u == 0:
            keep[flags_unit].wait()
            sf[0] = gf[pair_ref[0, 0]]
            sf[1] = gf[pair_ref[0, 1]]
            for k in range(1, hours):
                target = (me + k) % hours
                remote(sf, bf.at[me], f_send.at[k], f_recv.at[me], target)
            pltpu.make_async_copy(sf, bf.at[me], local_sem.at[3 + hours]).start()
        share(u)
        if u > 0:
            relay(u - 1)
    relay(hours - 1)

    for u in range(hours):
        span = pl.ds(u * part, part)
        for k in range(hours // CORES):
            peer = ((y + k) % (hours // CORES)) * CORES + (1 - core)
            got(j_recv.at[peer, u], bj.at[peer, span])
        pltpu.make_async_copy(sj.at[u], bj.at[me, span], local_sem.at[3 + u]).wait()
    for k in range(1, hours):
        peer = (me + k) % hours
        got(i_recv.at[peer], bi.at[peer])
        got(f_recv.at[peer], bf.at[peer])
    pltpu.make_async_copy(sf, bf.at[me], local_sem.at[3 + hours]).wait()
    pltpu.make_async_copy(si.at[0], bi.at[me], local_sem.at[2]).wait()
    for cond, make in pending:
        @pl.when(cond)
        def _(make=make):
            make().wait_send()
    for copy in late:
        copy.wait_send()


def exchange(pair_blocks, whitened, marks, pairs, width, hours):
    rows, cols = whitened.shape
    part = rows // hours
    any_space = pl.BlockSpec(memory_space=pl.ANY)
    dma = pltpu.SemaphoreType.DMA
    groups = hours // CORES
    return pl.pallas_call(
        functools.partial(exchange_kernel, pairs, width, hours),
        out_shape=(
            jax.ShapeDtypeStruct((hours, rows, cols), jnp.bfloat16),
            jax.ShapeDtypeStruct((hours, part, cols), jnp.bfloat16),
            jax.ShapeDtypeStruct((hours, 2) + marks.shape, jnp.bfloat16),
        ),
        in_specs=[pl.BlockSpec(memory_space=pltpu.SMEM), any_space, any_space],
        out_specs=(any_space, any_space, any_space),
        scratch_shapes=[pltpu.VMEM((pairs, part, cols), jnp.bfloat16)] * hours + [
            pltpu.VMEM((pairs,) + marks.shape, jnp.bfloat16),
            pltpu.VMEM((hours, part, cols), jnp.bfloat16),
            pltpu.VMEM((hours, part, cols), jnp.bfloat16),
            pltpu.VMEM((2,) + marks.shape, jnp.bfloat16),
            dma((4, pairs, hours + 1)),
            dma((pairs, hours + 1)),
            dma((groups, hours)),
            dma((hours, hours)),
            dma((groups, hours)),
            dma((hours,)),
            dma((hours,)),
            dma((hours,)),
            dma((hours,)),
            dma((hours + 4,)),
            dma((hours + 1,)),
        ],
        compiler_params=pltpu.CompilerParams(
            collective_id=0, has_side_effects=True, vmem_limit_bytes=32 << 20
        ),
        name="exchange",
    )(pair_blocks, whitened, marks)


GROUP = 8


def stack_kernel(hours, work, me_ref, bi_ref, bj_ref, bf_ref, g_ref, out_ref, af, cross, recip):
    step = pl.program_id(0)
    rows = bj_ref.shape[1]
    first_rows = bi_ref.shape[1]

    @pl.when(step == 0)
    def _():
        af[...] = bi_ref[...].astype(jnp.float32)
        first = bf_ref[:, 0, 0, :]
        second = bf_ref[:, 1, 0, :]
        counts = lax.dot_general(
            second, first, (((0,), (0,)), ((), ())), preferred_element_type=jnp.float32
        )
        recip[...] = 1.0 / jnp.maximum(counts, 1.0)

    block = 64
    for a in range(GROUP):
        row = pl.ds(pl.multiple_of(step * GROUP, GROUP), GROUP)
        for c in range(F // 128):
            lo, hi = c * 128, F + c * 128
            heads = []
            for h in range(hours):
                ar = af[h, row, lo : lo + 128][a : a + 1]
                ai = af[h, row, hi : hi + 128][a : a + 1]
                heads.append(
                    tuple(jnp.broadcast_to(t, (block, 128)).astype(work) for t in (ar, ai))
                )
            for r in range(0, rows, block):
                real = imag = None
                for h in range(hours):
                    ar, ai = heads[h]
                    br = bj_ref[h, r : r + block, lo : lo + 128].astype(work)
                    bm = bj_ref[h, r : r + block, hi : hi + 128].astype(work)
                    re = ar * br + ai * bm
                    im = ai * br - ar * bm
                    real = re if real is None else real + re
                    imag = im if imag is None else imag + im
                at = a * rows + r
                cross[at : at + block, lo : lo + 128] = real.astype(jnp.bfloat16)
                cross[at : at + block, hi : hi + 128] = imag.astype(jnp.bfloat16)
    lagged = jnp.dot(cross[...], g_ref[...], preferred_element_type=jnp.float32)
    offset = me_ref[0] * first_rows + step * GROUP
    scale = pltpu.roll(recip[...], (rows - offset) % rows, 1)
    for a in range(GROUP):
        out_ref[0, a] = lagged[a * rows : (a + 1) * rows] * scale[:, a : a + 1]


def stack(me, bi, bj, bf, weights, work):
    hours, first_rows, cols = bi.shape
    rows = bj.shape[1]
    full = lambda a: pl.BlockSpec(a.shape, lambda i, *_: (0,) * a.ndim, pipeline_mode=pl.Buffered(1))
    return pl.pallas_call(
        functools.partial(stack_kernel, hours, work),
        grid_spec=pltpu.PrefetchScalarGridSpec(
            num_scalar_prefetch=1,
            grid=(first_rows // GROUP,),
            in_specs=[full(bi), full(bj), full(bf), full(weights)],
            out_specs=pl.BlockSpec((1, GROUP, rows, LAGS), lambda i, *_: (0, i, 0, 0)),
            scratch_shapes=[
                pltpu.VMEM((hours, first_rows, cols), jnp.float32),
                pltpu.VMEM((GROUP * rows, cols), jnp.bfloat16),
                pltpu.VMEM((rows, rows), jnp.float32),
            ],
        ),
        out_shape=jax.ShapeDtypeStruct((1, first_rows, rows, LAGS), jnp.float32),
        compiler_params=pltpu.CompilerParams(vmem_limit_bytes=48 << 20),
        name="stack",
    )(me, bi, bj, bf, weights)


def whiten(records, usable):
    rows = records.shape[0]
    flat = records.reshape(rows, L).astype(jnp.float32)
    u = split_hi_lo(flat[:, :HALF] + flat[:, HALF:])
    v = split_hi_lo(flat[:, :HALF] - flat[:, HALF:])
    even, odd = spectrum_tables()
    flags = usable.astype(jnp.float32).reshape(rows, 1)
    return pl.pallas_call(
        whiten_kernel,
        out_shape=jax.ShapeDtypeStruct((rows, 2 * F), jnp.bfloat16),
        in_specs=[pl.BlockSpec(memory_space=pltpu.VMEM)] * 6,
        out_specs=pl.BlockSpec(memory_space=pltpu.VMEM),
        compiler_params=pltpu.CompilerParams(vmem_limit_bytes=48 << 20),
        name="whiten",
    )(u, v, flags, jnp.asarray(even), jnp.asarray(odd), jnp.asarray(window_ones()))


WORK = jnp.float32


def solution(mesh):
    pairs, hours = mesh.shape["pairs"], mesh.shape["hours"]
    width = 1 << ((pairs.bit_length() - 1) // 2)

    def body(records, usable, pair_blocks):
        rows = records.shape[0]
        whitened = whiten(records, usable)
        marks = jnp.broadcast_to(usable.astype(jnp.bfloat16).reshape(1, rows), (16, rows))
        bj, bi, bf = exchange(pair_blocks, whitened, marks, pairs, width, hours)
        me = lax.axis_index("hours").astype(jnp.int32).reshape(1)
        return stack(me, bi, bj, bf, jnp.asarray(lag_weights()), WORK)

    return jax.shard_map(
        body,
        mesh=mesh,
        in_specs=(P("pairs", "hours", None), P("pairs", "hours"), P("pairs", None)),
        out_specs=P("pairs", "hours", None, None),
        check_vma=False,
    )
```

time: 275 us -> 78.3 us (0.28)
  Pallas kernels: 0 us -> 73.3 us
  other arithmetic: 71.7 us -> 1.38 us
  waiting for transfers between devices: 61.4 us -> 0 us
  matrix products: 49.3 us -> 0 us
  local copies, waits for them, and re-layouts: 45.4 us -> 3.3 us
  blocking collectives: 23 us -> 0 us
  between operations: 13.5 us -> 0.08 us
  starting transfers between devices: 8.36 us -> 0 us
    pallas_call x0 -> x3, Pallas kernels: none -> 73.3 us  [the longest x1 53 us: exchange(): pl.pallas_call(functools.partial(exchange_kernel, pairs, width, hours), o...]
    another operation x6 -> x0, other arithmetic: 61.9 us -> none
    all_gather x2 -> x0, waiting for transfers between devices: 55.3 us -> none  [the longest x1 55.3 us: body(): lax.all_gather(records, 'pairs', axis=0, tiled=True)]
    dot_general x9 -> x0, matrix products: 49.3 us -> none  [the longest x4 34.9 us: add_hour(): jnp.dot(cross.reshape(first_rows * second_rows, 2 * F), weights, preferre...]
    all_gather x2 -> x0, blocking collectives: 23 us -> none  [the longest x1 17.9 us: body(): lax.all_gather(usable_marks, 'pairs', axis=0, tiled=True)]
    unnamed x8 -> x9, local copies, waits for them, and re-layouts: 17 us -> 3.18 us
    reshape x2 -> x0, local copies, waits for them, and re-layouts: 13.1 us -> none  [the longest x1 9.15 us: body(): pieces_in[0].reshape(block_count, -1)]
    all_gather x1 -> x0, local copies, waits for them, and re-layouts: 10.1 us -> none  [body(): lax.all_gather(records, 'pairs', axis=0, tiled=True)]
  transfers between devices with their start and end apart: 4 -> 0, of which waited for: 2 -> 0; matrix products, arithmetic and copies ran while one was open for 19% -> 0% of each run, Pallas kernels for 0% -> 0%
where the time goes in v1:
time: 78.3 us; the launch traced here: 78.1 us
  Pallas kernels  73.3 us (94%)
  local copies, waits for them, and re-layouts  3.3 us (4%)
  other arithmetic  1.38 us (2%)
    pallas_call x1, Pallas kernels, exchange(): pl.pallas_call(functools.partial(exchange_kernel, pairs, width, hours), o...  53 us
    pallas_call x1, Pallas kernels, stack(): pl.pallas_call(functools.partial(stack_kernel, hours, work), grid_spec=pl...  16.1 us
    pallas_call x1, Pallas kernels, whiten(): pl.pallas_call(whiten_kernel, out_shape=jax.ShapeDtypeStruct((rows, 2 * F...  4.23 us
    unnamed x9, local copies, waits for them, and re-layouts  3.18 us

profile of v1, /device:TPU:1, one launch (start us, length us, event | category | flops | bytes accessed | tf_op | source)
XLA Modules:
  0.0 78.1 jit_solution(11859952188898295358)
XLA Ops:
  0.0 0.7 convert_bitcast_fusion
  0.7 0.1 copy.11.flag_ref
  0.9 1.6 %copy.10 = bf16[128,1,3600]{2,0,1:T(8,128)(2,1)S(1)} copy(bf16[128,1,3600]{0,2,1:T(8,128)(2,1)} %param.7) | data formatting | bytes 1843200 | tf_op args[0]
  2.4 0.1 bitcast_convert_fusion
  2.6 0.4 subtract_convert_fusion
  3.0 0.0 copy-start
  3.0 0.0 copy-start.1
  3.0 0.1 pad_maximum_fusion
  3.1 1.5 %copy-done = bf16[1800,576]{1,0:T(8,128)(2,1)S(1)} copy-done((bf16[1800,576]{1,0:T(8,128)(2,1)S(1)}, bf16[1800,576]{1,0:T(8,128)(2,1)}, u32[]{:S(2)}) %copy-start) | copy-done | bytes 2073624
  4.6 0.1 copy-done.1
  4.7 0.0 copy-start.3
  4.7 0.0 copy-start.2
  4.7 4.2 %whiten.1.w_ref = bf16[128,1024]{1,0:T(8,128)(2,1)S(1)} custom-call(bf16[256,1800]{1,0:T(8,128)(2,1)S(1)} %get-tuple-element.19.u_ref, bf16[256,1800]{1,0:T(8,128)(2,1)S(1)} %get-tuple-element.20.v_ref, f32[128,1]{1,0:T(8,128)S(1)} %copy.11.flag_ref, bf16[1800,576]{1,0:T(8,128)(2,1)S(1)} %copy-done, bf16[1800,576]{1,0:T(8,128)(2,1)} %constant.13.clone.odd_ref, ...), custom_call_target="tpu_custom_call" | custom-call | tf_op jit(solution)/shard_map/whiten/pallas_call | solution.py:400
  9.0 0.0 copy-done.3
  9.0 53.0 %exchange.1 = (bf16[4,128,1024]{2,1,0:T(8,128)(2,1)S(1)}, bf16[4,32,1024]{2,1,0:T(8,128)(2,1)S(1)}, bf16[4,2,16,128]{3,2,1,0:T(8,128)(2,1)S(1)}) custom-call(s32[1,2]{1,0:T(1,128)S(1)} %copy-done.3, bf16[128,1024]{1,0:T(8,128)(2,1)S(1)} %whiten.1.w_ref, bf16[16,128]{1,0:T(8,128)(2,1)S(1)} %broadcast_in_dim.8.f_ref), custom_call_target="tpu_custom_call" | custom-call | tf_op jit(solution)/shard_map/exchange/pallas_call | solution.py:287
  62.0 0.0 copy-done.2
  62.0 16.1 %stack.1 = f32[1,32,128,256]{3,2,1,0:T(8,128)} custom-call(s32[1]{0:T(128)} %bitcast.me_ref, bf16[4,32,1024]{2,1,0:T(8,128)(2,1)S(1)} %get-tuple-element.8.bi_ref, bf16[4,128,1024]{2,1,0:T(8,128)(2,1)S(1)} %get-tuple-element.9.bj_ref, bf16[4,2,16,128]{3,2,1,0:T(8,128)(2,1)S(1)} %get-tuple-element.10.bf_ref, bf16[1024,256]{1,0:T(8,128)(2,1)S(1)} %copy-done.2), custom_call_target="tpu_custom_call" | custom-call | tf_op jit(solution)/shard_map/stack/pallas_call | solution.py:374
  (1 shorter events, 0.0 us)
Async XLA Ops:
  3.0 1.7 %copy-start = (bf16[1800,576]{1,0:T(8,128)(2,1)S(1)}, bf16[1800,576]{1,0:T(8,128)(2,1)}, u32[]{:S(2)}) copy-start(bf16[1800,576]{1,0:T(8,128)(2,1)} %constant.12.clone.even_ref) | copy-start | bytes 6220804
  3.0 1.7 %copy-start.1 = (bf16[576,512]{1,0:T(8,128)(2,1)S(1)}, bf16[576,512]{1,0:T(8,128)(2,1)}, u32[]{:S(2)}) copy-start(bf16[576,512]{1,0:T(8,128)(2,1)} %constant.14.clone.ones_ref) | copy-start | bytes 1769476
  4.7 4.2 %copy-start.3 = (s32[1,2]{1,0:T(1,128)S(1)}, s32[1,2]{1,0:T(1,128)}, u32[]{:S(2)}) copy-start(s32[1,2]{1,0:T(1,128)} %pair_ref.1) | copy-start | bytes 28
  4.7 57.3 %copy-start.2 = (bf16[1024,256]{1,0:T(8,128)(2,1)S(1)}, bf16[1024,256]{1,0:T(8,128)(2,1)}, u32[]{:S(2)}) copy-start(bf16[1024,256]{1,0:T(8,128)(2,1)} %constant.15.clone.g_ref) | copy-start | bytes 1572868

commit v2 on v1

v2 whole, which is shorter than its diff:
```python
import functools
import math

import jax
import jax.numpy as jnp
import numpy as np
from jax import lax
from jax.experimental import pallas as pl
from jax.experimental.pallas import tpu as pltpu
from jax.sharding import PartitionSpec as P

L = 3600
F = 512
W = 32
F0 = 64
LAGS = 256
EXTENT = F + 2 * W
HALF = L // 2
HE = EXTENT // 2
HF = F // 2
CORES = 2
MESH = pl.DeviceIdType.MESH


def cos_sin(phases, length, scale):
    angles = np.float32(2.0 * math.pi / length) * (phases % length).astype(np.float32)
    wide = angles.astype(np.float64)
    scale = np.float32(scale)
    return np.cos(wide).astype(np.float32) * scale, -np.sin(wide).astype(np.float32) * scale


CHUNK = 128
CHUNKS = F // CHUNK


def spectrum_tables():
    bins = F0 - W + np.arange(EXTENT)
    c, q = cos_sin(bins[:, None] * np.arange(HALF)[None, :], L, 1.0 / math.sqrt(L))
    even = np.concatenate([c[0::2], q[0::2]], axis=0)
    odd = np.concatenate([c[1::2], q[1::2]], axis=0)
    return even.astype(jnp.bfloat16), odd.astype(jnp.bfloat16)


def window_ones():
    source = np.concatenate([np.arange(0, EXTENT, 2), np.arange(1, EXTENT, 2)])
    target = np.concatenate([np.arange(0, F, 2), np.arange(1, F, 2)])
    gap = source[None, :] - target[:, None]
    return ((gap >= 0) & (gap <= 2 * W)).astype(np.float32).astype(jnp.bfloat16)


def lag_weights():
    order = np.concatenate([np.arange(0, F, 2), np.arange(1, F, 2)])
    shifts = np.arange(LAGS) - LAGS // 2
    c, s = cos_sin((F0 + order)[:, None] * shifts[None, :], L, 1.0 / math.sqrt(F))
    pieces = []
    for k in range(0, F, CHUNK):
        pieces += [c[k : k + CHUNK], s[k : k + CHUNK]]
    return np.concatenate(pieces, axis=0).astype(jnp.bfloat16)


def split_hi_lo(value):
    high = value.astype(jnp.bfloat16)
    low = (value - high.astype(jnp.float32)).astype(jnp.bfloat16)
    return jnp.concatenate([high, low], axis=1)


def whiten_kernel(
    x_ref, use_ref, even_hbm, odd_hbm, ones_hbm, out_ref, mark_ref, even, odd, ones, sem
):
    stations = x_ref.shape[1]
    loads = [
        pltpu.make_async_copy(src, dst, sem.at[k])
        for k, (src, dst) in enumerate(((even_hbm, even), (odd_hbm, odd), (ones_hbm, ones)))
    ]
    for load in loads:
        load.start()
    flags = use_ref[...].astype(jnp.float32)
    mark_ref[...] = jnp.broadcast_to(flags, mark_ref.shape).astype(jnp.bfloat16)
    early = x_ref[:HALF].astype(jnp.float32)
    late = x_ref[HALF:].astype(jnp.float32)

    def transform(load, table, signal):
        signal = split_hi_lo(signal)
        load.wait()
        both = jnp.dot(table[...], signal, preferred_element_type=jnp.float32)
        both = both[:, :stations] + both[:, stations:]
        return both[:HE], both[HE:]

    re_even, im_even = transform(loads[0], even, early + late)
    re_odd, im_odd = transform(loads[1], odd, early - late)
    power = jnp.concatenate(
        [re_even * re_even + im_even * im_even, re_odd * re_odd + im_odd * im_odd], axis=0
    )
    loads[2].wait()
    total = jnp.dot(ones[...], split_hi_lo(power), preferred_element_type=jnp.float32)
    smooth = (total[:, :stations] + total[:, stations:]) * jnp.float32(1.0 / (2 * W + 1))
    weight = flags / jnp.sqrt(smooth + 1e-05)
    w2 = W // 2
    for k in range(CHUNKS):
        at = k * CHUNK
        real, imag = (re_even, im_even) if at < HF else (re_odd, im_odd)
        inner = w2 + at % HF
        scale = weight[at : at + CHUNK]
        out_ref[k, :, :CHUNK] = (real[inner : inner + CHUNK] * scale).T.astype(jnp.bfloat16)
        out_ref[k, :, CHUNK:] = (imag[inner : inner + CHUNK] * scale).T.astype(jnp.bfloat16)


def exchange_kernel(
    pairs, width, hours, pair_ref, w_ref, f_ref, bj, bi, bf,
    *scratch,
):
    rows = w_ref.shape[1]
    part = rows // hours
    span_rows = rows // SPLIT
    units = CHUNKS * SPLIT
    g = scratch[:units]
    (
        gf, sj, si, sf, zx_send, zx_recv, j_send, j_recv, relay_send, i_send, i_recv,
        f_send, f_recv, local_sem, i_local,
    ) = scratch[units:]
    depth = pairs // width
    p = lax.axis_index("pairs")
    me = lax.axis_index("hours")
    z, x = p // width, p % width
    y, core = me // CORES, me % CORES
    partner = y * CORES + (1 - core)
    flags_unit = units

    def place(u):
        return u // SPLIT, pl.ds((u % SPLIT) * span_rows, span_rows)

    steps = (
        (z + 1 < depth, p + width),
        (z > 0, p - width),
        (x + 1 < width, p + 1),
        (x > 0, p - 1),
    )

    barrier = pltpu.get_barrier_semaphore()
    for exists, target in steps:
        @pl.when(exists)
        def _(target=target):
            pl.semaphore_signal(barrier, inc=1, device_id={"pairs": target}, device_id_type=MESH)
    for k in range(1, hours):
        pl.semaphore_signal(
            barrier, inc=1, device_id={"hours": (me + k) % hours}, device_id_type=MESH
        )
    near = sum(e.astype(jnp.int32) for e, _ in steps)
    pl.semaphore_wait(barrier, near + hours - 1)

    pending = []

    def slot(b, u):
        return gf.at[b] if u == flags_unit else g[u].at[b]

    def own(u):
        return f_ref if u == flags_unit else w_ref.at[place(u)]

    def forward(cond, b, u, way, is_own=False):
        exists, target = steps[way]
        both = exists if cond is None else jnp.logical_and(cond, exists)

        def make():
            return pltpu.make_async_remote_copy(
                src_ref=own(u) if is_own else slot(b, u),
                dst_ref=slot(b, u),
                send_sem=zx_send.at[way, b, u],
                recv_sem=zx_recv.at[b, u],
                device_id={"pairs": target},
                device_id_type=MESH,
            )

        @pl.when(both)
        def _():
            make().start()
        pending.append((both, make))

    def arrived(b, u):
        pltpu.make_async_remote_copy(
            src_ref=slot(b, u), dst_ref=slot(b, u), send_sem=zx_send.at[0, b, u],
            recv_sem=zx_recv.at[b, u], device_id={"pairs": p}, device_id_type=MESH,
        ).wait_recv()

    def send_own(u):
        for way in range(4):
            forward(None, p, u, way, is_own=True)

    keep = [
        pltpu.make_async_copy(own(u), slot(p, u), local_sem.at[u]) for u in range(units + 1)
    ]
    for copy in keep:
        copy.start()

    def gather_z(u, d):
        for way, b, cond in (
            (0, p - d * width, z - d >= 0),
            (1, p + d * width, z + d < depth),
        ):
            @pl.when(cond)
            def _(b=b):
                arrived(b, u)
            for out in (way, 2, 3):
                forward(cond, b, u, out)

    def gather_x(u):
        for d in range(1, width):
            for zz in range(depth):
                for way, b, cond in (
                    (2, zz * width + x - d, x - d >= 0),
                    (3, zz * width + x + d, x + d < width),
                ):
                    @pl.when(cond)
                    def _(b=b):
                        arrived(b, u)
                    if width > 2:
                        forward(cond, b, u, way)

    late = []
    local = []

    def remote(src, dst, send_sem, recv_sem, target):
        copy = pltpu.make_async_remote_copy(
            src_ref=src, dst_ref=dst, send_sem=send_sem, recv_sem=recv_sem,
            device_id={"hours": target}, device_id_type=MESH,
        )
        copy.start()
        late.append(copy)

    def stay(src, dst, sem):
        copy = pltpu.make_async_copy(src, dst, sem)
        copy.start()
        local.append(copy)

    def share(u):
        keep[u].wait()
        if u == flags_unit:
            sf[0] = gf[pair_ref[0, 0]]
            sf[1] = gf[pair_ref[0, 1]]
            for k in range(1, hours):
                remote(sf, bf.at[me], f_send.at[k], f_recv.at[me], (me + k) % hours)
            stay(sf, bf.at[me], local_sem.at[units + 1])
            return
        c, span = place(u)
        sj[u] = g[u][pair_ref[0, 1]]
        si[u] = g[u][pair_ref[0, 0]]
        for k in range(1, hours // CORES):
            target = ((y + k) % (hours // CORES)) * CORES + core
            remote(sj.at[u], bj.at[me, c, span], j_send.at[k, u], j_recv.at[me, u], target)
        remote(sj.at[u], bj.at[me, c, span], j_send.at[0, u], j_recv.at[me, u], partner)
        stay(sj.at[u], bj.at[me, c, span], local_sem.at[units + 2 + u])
        share_hours = hours // SPLIT
        for k in range(share_hours):
            peer = (u % SPLIT) * share_hours + k
            rows_of = si.at[u, pl.ds(k * part, part)]

            def make(peer=peer, rows_of=rows_of):
                return pltpu.make_async_remote_copy(
                    src_ref=rows_of, dst_ref=bi.at[me, c], send_sem=i_send.at[c, peer],
                    recv_sem=i_recv.at[me, c], device_id={"hours": peer}, device_id_type=MESH,
                )

            @pl.when(me != peer)
            def _(make=make):
                make().start()
            pending.append((me != peer, make))

            @pl.when(me == peer)
            def _(rows_of=rows_of):
                pltpu.make_async_copy(rows_of, bi.at[me, c], i_local.at[c]).start()

    def got(sem, ref):
        pltpu.make_async_remote_copy(
            src_ref=ref, dst_ref=ref, send_sem=sem, recv_sem=sem,
            device_id={"hours": me}, device_id_type=MESH,
        ).wait_recv()

    def relay(u):
        c, span = place(u)
        for k in range(1, hours // CORES):
            peer = ((y + k) % (hours // CORES)) * CORES + core
            piece = bj.at[peer, c, span]
            got(j_recv.at[peer, u], piece)
            remote(piece, piece, relay_send.at[k, u], j_recv.at[peer, u], partner)

    order = [flags_unit] + list(range(units))
    for t in range(len(order) + depth + 2):
        if t < len(order):
            for way in (2, 0, 1, 3):
                forward(None, p, order[t], way, is_own=True)
        for d in range(1, depth):
            if 0 <= t - d < len(order):
                gather_z(order[t - d], d)
        if 0 <= t - depth < len(order):
            gather_x(order[t - depth])
            share(order[t - depth])
        if 1 <= t - depth - 2 < len(order):
            relay(order[t - depth - 2])

    for u in range(units):
        c, span = place(u)
        for k in range(hours // CORES):
            peer = ((y + k) % (hours // CORES)) * CORES + (1 - core)
            got(j_recv.at[peer, u], bj.at[peer, c, span])
    for k in range(1, hours):
        peer = (me + k) % hours
        for c in range(CHUNKS):
            got(i_recv.at[peer, c], bi.at[peer, c])
        got(f_recv.at[peer], bf.at[peer])
    for copy in local:
        copy.wait()
    for c in range(CHUNKS):
        pltpu.make_async_copy(bi.at[me, c], bi.at[me, c], i_local.at[c]).wait()
    for cond, make in pending:
        @pl.when(cond)
        def _(make=make):
            make().wait_send()
    for copy in late:
        copy.wait_send()


SPLIT = 2


def exchange(pair_blocks, whitened, marks, pairs, width, hours):
    rows, cols = whitened.shape[1:]
    part = rows // hours
    units = CHUNKS * SPLIT
    any_space = pl.BlockSpec(memory_space=pl.ANY)
    dma = pltpu.SemaphoreType.DMA
    groups = hours // CORES
    return pl.pallas_call(
        functools.partial(exchange_kernel, pairs, width, hours),
        out_shape=(
            jax.ShapeDtypeStruct((hours, CHUNKS, rows, cols), jnp.bfloat16),
            jax.ShapeDtypeStruct((hours, CHUNKS, part, cols), jnp.bfloat16),
            jax.ShapeDtypeStruct((hours, 2) + marks.shape, jnp.bfloat16),
        ),
        in_specs=[pl.BlockSpec(memory_space=pltpu.SMEM), any_space, any_space],
        out_specs=(any_space, any_space, any_space),
        scratch_shapes=[pltpu.VMEM((pairs, rows // SPLIT, cols), jnp.bfloat16)] * units + [
            pltpu.VMEM((pairs,) + marks.shape, jnp.bfloat16),
            pltpu.VMEM((units, rows // SPLIT, cols), jnp.bfloat16),
            pltpu.VMEM((units, rows // SPLIT, cols), jnp.bfloat16),
            pltpu.VMEM((2,) + marks.shape, jnp.bfloat16),
            dma((4, pairs, units + 1)),
            dma((pairs, units + 1)),
            dma((groups, units)),
            dma((hours, units)),
            dma((groups, units)),
            dma((CHUNKS, hours)),
            dma((hours, CHUNKS)),
            dma((hours,)),
            dma((hours,)),
            dma((2 * units + 2,)),
            dma((CHUNKS,)),
        ],
        compiler_params=pltpu.CompilerParams(
            collective_id=0, has_side_effects=True, vmem_limit_bytes=32 << 20
        ),
        name="exchange",
    )(pair_blocks, whitened, marks)


GROUP = 8
SUB = 2
BLOCK = 16


def stack_kernel(
    hours, me_ref, bi_ref, bj_ref, bf_ref, g_ref, out_ref, af, heads, recip, *cross
):
    step = pl.program_id(0)
    rows = bj_ref.shape[2]
    first_rows = bi_ref.shape[2]
    f32 = jnp.float32

    @pl.when(step == 0)
    def _():
        af[...] = bi_ref[...].astype(f32)
        first = bf_ref[:, 0, 0, :]
        second = bf_ref[:, 1, 0, :]
        counts = lax.dot_general(
            second, first, (((0,), (0,)), ((), ())), preferred_element_type=f32
        )
        recip[...] = 1.0 / jnp.maximum(counts, 1.0)

    offset = me_ref[0] * first_rows + step * GROUP
    scale = pltpu.roll(recip[...], (rows - offset) % rows, 1)
    at_rows = pl.ds(pl.multiple_of(step * GROUP, GROUP), GROUP)
    for h in range(hours):
        for c in range(CHUNKS):
            ar = af[h, c, at_rows, :CHUNK]
            ai = af[h, c, at_rows, CHUNK:]
            for k, value in enumerate((ar, ar + ai, ai - ar)):
                for a in range(GROUP):
                    heads[a, c, h, k] = jnp.broadcast_to(value[a : a + 1], (8, CHUNK))

    def wide(value):
        return jnp.concatenate([value] * (BLOCK // 8), axis=0)

    for sub in range(GROUP // SUB):
        buf = cross[sub]
        for c in range(CHUNKS):
            lo = 2 * CHUNK * c
            hi = lo + CHUNK
            for r in range(0, rows, BLOCK):
                tails = []
                for h in range(hours):
                    br = bj_ref[h, c, r : r + BLOCK, :CHUNK].astype(f32)
                    bm = bj_ref[h, c, r : r + BLOCK, CHUNK:].astype(f32)
                    tails.append((br - bm, bm, br))
                for a in range(SUB):
                    sums = [None, None, None]
                    for h in range(hours):
                        for k in range(3):
                            term = wide(heads[sub * SUB + a, c, h, k]) * tails[h][k]
                            sums[k] = term if sums[k] is None else sums[k] + term
                    at = a * rows + r
                    buf[at : at + BLOCK, lo:hi] = (sums[0] + sums[1]).astype(jnp.bfloat16)
                    buf[at : at + BLOCK, hi : hi + CHUNK] = (sums[0] + sums[2]).astype(
                        jnp.bfloat16
                    )
        lagged = jnp.dot(buf[...], g_ref[...], preferred_element_type=f32)
        for a in range(SUB):
            k = sub * SUB + a
            out_ref[0, k] = lagged[a * rows : (a + 1) * rows] * scale[:, k : k + 1]


def stack(me, bi, bj, bf, weights):
    hours, _, first_rows, cols = bi.shape
    rows = bj.shape[2]
    full = lambda a: pl.BlockSpec(a.shape, lambda i, *_: (0,) * a.ndim, pipeline_mode=pl.Buffered(1))
    return pl.pallas_call(
        functools.partial(stack_kernel, hours),
        grid_spec=pltpu.PrefetchScalarGridSpec(
            num_scalar_prefetch=1,
            grid=(first_rows // GROUP,),
            in_specs=[full(bi), full(bj), full(bf), full(weights)],
            out_specs=pl.BlockSpec((1, GROUP, rows, LAGS), lambda i, *_: (0, i, 0, 0)),
            scratch_shapes=[
                pltpu.VMEM((hours, CHUNKS, first_rows, cols), jnp.float32),
                pltpu.VMEM((GROUP, CHUNKS, hours, 3, 8, CHUNK), jnp.float32),
                pltpu.VMEM((rows, rows), jnp.float32),
            ]
            + [pltpu.VMEM((SUB * rows, 2 * F), jnp.bfloat16)] * (GROUP // SUB),
        ),
        out_shape=jax.ShapeDtypeStruct((1, first_rows, rows, LAGS), jnp.float32),
        compiler_params=pltpu.CompilerParams(vmem_limit_bytes=48 << 20),
        name="stack",
    )(me, bi, bj, bf, weights)


def whiten(records, usable):
    rows = records.shape[0]
    samples = records.reshape(rows, L).T
    even, odd = spectrum_tables()
    tables = (jnp.asarray(even), jnp.asarray(odd), jnp.asarray(window_ones()))
    vmem = pl.BlockSpec(memory_space=pltpu.VMEM)
    hbm = pl.BlockSpec(memory_space=pltpu.HBM)
    return pl.pallas_call(
        whiten_kernel,
        out_shape=(
            jax.ShapeDtypeStruct((CHUNKS, rows, 2 * CHUNK), jnp.bfloat16),
            jax.ShapeDtypeStruct((16, rows), jnp.bfloat16),
        ),
        in_specs=[vmem, vmem, hbm, hbm, hbm],
        out_specs=(vmem, vmem),
        scratch_shapes=[pltpu.VMEM(t.shape, t.dtype) for t in tables]
        + [pltpu.SemaphoreType.DMA((3,))],
        compiler_params=pltpu.CompilerParams(vmem_limit_bytes=48 << 20),
        name="whiten",
    )(samples, usable.reshape(1, rows), *tables)


def solution(mesh):
    pairs, hours = mesh.shape["pairs"], mesh.shape["hours"]
    width = 1 << ((pairs.bit_length() - 1) // 2)

    def body(records, usable, pair_blocks):
        whitened, marks = whiten(records, usable)
        bj, bi, bf = exchange(pair_blocks, whitened, marks, pairs, width, hours)
        me = lax.axis_index("hours").astype(jnp.int32).reshape(1)
        return stack(me, bi, bj, bf, jnp.asarray(lag_weights()))

    return jax.shard_map(
        body,
        mesh=mesh,
        in_specs=(P("pairs", "hours", None), P("pairs", "hours"), P("pairs", None)),
        out_specs=P("pairs", "hours", None, None),
        check_vma=False,
    )
```

time: 78.3 us -> 65.7 us (0.84)
  Pallas kernels: 73.3 us -> 60.9 us
  other arithmetic: 1.38 us -> 0 us
  local copies, waits for them, and re-layouts: 3.3 us -> 4.55 us
    pallas_call x1, Pallas kernels: 53 us -> 44.7 us  [exchange(): pl.pallas_call(functools.partial(exchange_kernel, pairs, width, hours), o...]
    pallas_call x2, Pallas kernels: 20.3 us -> 16.2 us  [the longest x1 12.1 us: stack(): pl.pallas_call(functools.partial(stack_kernel, hours), grid_spec=pltpu.Pr...]
    unnamed x9 -> x12, local copies, waits for them, and re-layouts: 3.18 us -> 4.55 us
where the time goes in v2:
time: 65.7 us; the launch traced here: 65.5 us
  Pallas kernels  60.9 us (93%)
  local copies, waits for them, and re-layouts  4.55 us (7%)
    pallas_call x1, Pallas kernels, exchange(): pl.pallas_call(functools.partial(exchange_kernel, pairs, width, hours), o...  44.7 us
    pallas_call x1, Pallas kernels, stack(): pl.pallas_call(functools.partial(stack_kernel, hours), grid_spec=pltpu.Pr...  12.1 us
    unnamed x12, local copies, waits for them, and re-layouts  4.55 us
    pallas_call x1, Pallas kernels, whiten(): pl.pallas_call(whiten_kernel, out_shape=(jax.ShapeDtypeStruct((CHUNKS, ro...  4.16 us

profile of v2, /device:TPU:1, one launch (start us, length us, event | category | flops | bytes accessed | tf_op | source)
XLA Modules:
  0.0 65.5 jit_solution(10270072609079979730)
XLA Ops:
  0.0 0.0 copy-start
  0.0 1.6 %copy-done = bf16[576,1800]{1,0:T(8,128)(2,1)S(1)} copy-done((bf16[576,1800]{1,0:T(8,128)(2,1)S(1)}, bf16[576,1800]{1,0:T(8,128)(2,1)}, u32[]{:S(2)}) %copy-start) | copy-done | bytes 2073624
  1.6 0.0 copy-start.1
  1.6 1.2 %copy-done.1 = bf16[128,1,3600]{0,2,1:T(8,128)(2,1)S(1)} copy-done((bf16[128,1,3600]{0,2,1:T(8,128)(2,1)S(1)}, bf16[128,1,3600]{0,2,1:T(8,128)(2,1)}, u32[]{:S(2)}) %copy-start.1) | copy-done | bytes 921624
  2.8 0.0 copy-start.2
  2.8 1.1 %copy-done.2 = bf16[512,576]{1,0:T(8,128)(2,1)S(1)} copy-done((bf16[512,576]{1,0:T(8,128)(2,1)S(1)}, bf16[512,576]{1,0:T(8,128)(2,1)}, u32[]{:S(2)}) %copy-start.2) | copy-done | bytes 589848
  3.9 0.0 copy-start.5
  3.9 0.7 copy-done.5
  4.5 0.0 copy-start.4
  4.6 0.0 copy-start.3
  4.6 4.2 %whiten.1 = (bf16[4,128,256]{2,1,0:T(8,128)(2,1)S(1)}, bf16[16,128]{1,0:T(8,128)(2,1)S(1)}) custom-call(bf16[3600,128]{1,0:T(8,128)(2,1)S(1)} %bitcast.5, s32[1,128]{1,0:T(1,128)S(1)} %bitcast.6, bf16[576,1800]{1,0:T(8,128)(2,1)S(1)} %copy-done, bf16[576,1800]{1,0:T(8,128)(2,1)} %constant.13.clone.odd_hbm, bf16[512,576]{1,0:T(8,128)(2,1)S(1)} %copy-done.2), custom_call_target="tpu_custom_call" | custom-call | tf_op jit(solution)/shard_map/whiten/pallas_call | solution.py:460
  8.7 0.0 copy-done.4
  8.7 44.7 %exchange.1 = (bf16[4,4,128,256]{3,2,1,0:T(8,128)(2,1)S(1)}, bf16[4,4,32,256]{3,2,1,0:T(8,128)(2,1)S(1)}, bf16[4,2,16,128]{3,2,1,0:T(8,128)(2,1)S(1)}) custom-call(s32[1,2]{1,0:T(1,128)S(1)} %copy-done.4, bf16[4,128,256]{2,1,0:T(8,128)(2,1)S(1)} %get-tuple-element.10.w_ref, bf16[16,128]{1,0:T(8,128)(2,1)S(1)} %get-tuple-element.11.f_ref), custom_call_target="tpu_custom_call" | custom-call | tf_op jit(solution)/shard_map/exchange/pallas_call | solution.py:331
  53.4 0.0 copy-done.3
  53.4 12.1 %stack.1 = f32[1,32,128,256]{3,2,1,0:T(8,128)} custom-call(s32[1]{0:T(128)} %bitcast.me_ref, bf16[4,4,32,256]{3,2,1,0:T(8,128)(2,1)S(1)} %get-tuple-element.12.bi_ref, bf16[4,4,128,256]{3,2,1,0:T(8,128)(2,1)S(1)} %get-tuple-element.13.bj_ref, bf16[4,2,16,128]{3,2,1,0:T(8,128)(2,1)S(1)} %get-tuple-element.14.bf_ref, bf16[1024,256]{1,0:T(8,128)(2,1)S(1)} %copy-done.3), custom_call_target="tpu_custom_call" | custom-call | tf_op jit(solution)/shard_map/stack/pallas_call | solution.py:433
Async XLA Ops:
  0.0 1.6 %copy-start = (bf16[576,1800]{1,0:T(8,128)(2,1)S(1)}, bf16[576,1800]{1,0:T(8,128)(2,1)}, u32[]{:S(2)}) copy-start(bf16[576,1800]{1,0:T(8,128)(2,1)} %constant.12.clone.even_hbm) | copy-start | bytes 6220804
  1.6 1.2 %copy-start.1 = (bf16[128,1,3600]{0,2,1:T(8,128)(2,1)S(1)}, bf16[128,1,3600]{0,2,1:T(8,128)(2,1)}, u32[]{:S(2)}) copy-start(bf16[128,1,3600]{0,2,1:T(8,128)(2,1)} %param.7) | copy-start | bytes 2764804
  2.8 1.1 %copy-start.2 = (bf16[512,576]{1,0:T(8,128)(2,1)S(1)}, bf16[512,576]{1,0:T(8,128)(2,1)}, u32[]{:S(2)}) copy-start(bf16[512,576]{1,0:T(8,128)(2,1)} %constant.14.clone.ones_hbm) | copy-start | bytes 1769476
  3.9 0.7 %copy-start.5 = (s32[128,1]{0,1:T(1,128)S(1)}, s32[128,1]{0,1:T(1,128)}, u32[]{:S(2)}) copy-start(s32[128,1]{0,1:T(1,128)} %param.8) | copy-start | bytes 1540
  4.5 4.2 %copy-start.4 = (s32[1,2]{1,0:T(1,128)S(1)}, s32[1,2]{1,0:T(1,128)}, u32[]{:S(2)}) copy-start(s32[1,2]{1,0:T(1,128)} %pair_ref.1) | copy-start | bytes 28
  4.6 48.9 %copy-start.3 = (bf16[1024,256]{1,0:T(8,128)(2,1)S(1)}, bf16[1024,256]{1,0:T(8,128)(2,1)}, u32[]{:S(2)}) copy-start(bf16[1024,256]{1,0:T(8,128)(2,1)} %constant.15.clone.g_ref) | copy-start | bytes 1572868

commit v3 on v2

--- a/solution.py
+++ b/solution.py
@@ -106,7 +106,7 @@
 
 
 def exchange_kernel(
-    pairs, width, hours, pair_ref, w_ref, f_ref, bj, bi, bf,
+    pairs, width, hours, pair_ref, ask_ref, w_ref, f_ref, bj, bi, bf,
     *scratch,
 ):
     rows = w_ref.shape[1]
@@ -115,8 +115,8 @@
     units = CHUNKS * SPLIT
     g = scratch[:units]
     (
-        gf, sj, si, sf, zx_send, zx_recv, j_send, j_recv, relay_send, i_send, i_recv,
-        f_send, f_recv, local_sem, i_local,
+        gf, sj, si, sf, hand, hand_f, asks, zx_send, zx_recv, j_send, j_recv, relay_send,
+        i_send, i_recv, f_send, f_recv, local_sem, i_local, a_send, a_recv, x_send, x_recv,
     ) = scratch[units:]
     depth = pairs // width
     p = lax.axis_index("pairs")
@@ -129,11 +129,12 @@
     def place(u):
         return u // SPLIT, pl.ds((u % SPLIT) * span_rows, span_rows)
 
+    def beside(k):
+        return z * width + (x + k) % width
+
     steps = (
         (z + 1 < depth, p + width),
         (z > 0, p - width),
-        (x + 1 < width, p + 1),
-        (x > 0, p - 1),
     )
 
     barrier = pltpu.get_barrier_semaphore()
@@ -145,13 +146,17 @@
         pl.semaphore_signal(
             barrier, inc=1, device_id={"hours": (me + k) % hours}, device_id_type=MESH
         )
+    for k in range(1, width):
+        pl.semaphore_signal(
+            barrier, inc=1, device_id={"pairs": beside(k)}, device_id_type=MESH
+        )
     near = sum(e.astype(jnp.int32) for e, _ in steps)
-    pl.semaphore_wait(barrier, near + hours - 1)
+    pl.semaphore_wait(barrier, near + hours - 1 + width - 1)
 
     pending = []
 
     def slot(b, u):
-        return gf.at[b] if u == flags_unit else g[u].at[b]
+        return gf.at[b // width] if u == flags_unit else g[u].at[b // width]
 
     def own(u):
         return f_ref if u == flags_unit else w_ref.at[place(u)]
@@ -164,8 +169,8 @@
             return pltpu.make_async_remote_copy(
                 src_ref=own(u) if is_own else slot(b, u),
                 dst_ref=slot(b, u),
-                send_sem=zx_send.at[way, b, u],
-                recv_sem=zx_recv.at[b, u],
+                send_sem=zx_send.at[way, b // width, u],
+                recv_sem=zx_recv.at[b // width, u],
                 device_id={"pairs": target},
                 device_id_type=MESH,
             )
@@ -177,8 +182,8 @@
 
     def arrived(b, u):
         pltpu.make_async_remote_copy(
-            src_ref=slot(b, u), dst_ref=slot(b, u), send_sem=zx_send.at[0, b, u],
-            recv_sem=zx_recv.at[b, u], device_id={"pairs": p}, device_id_type=MESH,
+            src_ref=slot(b, u), dst_ref=slot(b, u), send_sem=zx_send.at[0, b // width, u],
+            recv_sem=zx_recv.at[b // width, u], device_id={"pairs": p}, device_id_type=MESH,
         ).wait_recv()
 
     def send_own(u):
@@ -199,21 +204,41 @@
             @pl.when(cond)
             def _(b=b):
                 arrived(b, u)
-            for out in (way, 2, 3):
-                forward(cond, b, u, out)
-
-    def gather_x(u):
-        for d in range(1, width):
-            for zz in range(depth):
-                for way, b, cond in (
-                    (2, zz * width + x - d, x - d >= 0),
-                    (3, zz * width + x + d, x + d < width),
-                ):
-                    @pl.when(cond)
-                    def _(b=b):
-                        arrived(b, u)
-                    if width > 2:
-                        forward(cond, b, u, way)
+            forward(cond, b, u, way)
+
+    def crossing(k, u):
+        hand_of = hand_f.at[k - 1] if u == flags_unit else hand.at[k - 1, u]
+        dst = gf if u == flags_unit else g[u]
+        return pltpu.make_async_remote_copy(
+            src_ref=hand_of,
+            dst_ref=dst.at[pl.ds(depth + 2 * (width - k - 1), 2)],
+            send_sem=x_send.at[k - 1, u],
+            recv_sem=x_recv.at[width - k - 1, u],
+            device_id={"pairs": beside(k)},
+            device_id_type=MESH,
+        )
+
+    def offer(u):
+        keep[u].wait()
+        pool = gf if u == flags_unit else g[u]
+        for k in range(1, width):
+            for s in range(2):
+                asked = asks[k - 1, s, 0:1, 0:1].astype(jnp.float32)
+                picked = None
+                for zz in range(depth):
+                    mark = jnp.where(asked == (zz * width + x).astype(jnp.float32), 1.0, 0.0)
+                    term = pool[zz].astype(jnp.float32) * mark
+                    picked = term if picked is None else picked + term
+                if u == flags_unit:
+                    hand_f[k - 1, s] = picked.astype(jnp.bfloat16)
+                else:
+                    hand[k - 1, u, s] = picked.astype(jnp.bfloat16)
+            crossing(k, u).start()
+
+    def chosen(s):
+        b = pair_ref[0, s]
+        away = lax.rem(lax.rem(b, width) - x + width, width)
+        return jnp.where(away == 0, b // width, depth + 2 * (away - 1) + s)
 
     late = []
     local = []
@@ -232,17 +257,18 @@
         local.append(copy)
 
     def share(u):
-        keep[u].wait()
+        for k in range(1, width):
+            crossing(width - k, u).wait_recv()
         if u == flags_unit:
-            sf[0] = gf[pair_ref[0, 0]]
-            sf[1] = gf[pair_ref[0, 1]]
+            sf[0] = gf[chosen(0)]
+            sf[1] = gf[chosen(1)]
             for k in range(1, hours):
                 remote(sf, bf.at[me], f_send.at[k], f_recv.at[me], (me + k) % hours)
             stay(sf, bf.at[me], local_sem.at[units + 1])
             return
         c, span = place(u)
-        sj[u] = g[u][pair_ref[0, 1]]
-        si[u] = g[u][pair_ref[0, 0]]
+        sj[u] = g[u][chosen(1)]
+        si[u] = g[u][chosen(0)]
         for k in range(1, hours // CORES):
             target = ((y + k) % (hours // CORES)) * CORES + core
             remote(sj.at[u], bj.at[me, c, span], j_send.at[k, u], j_recv.at[me, u], target)
@@ -282,20 +308,37 @@
             got(j_recv.at[peer, u], piece)
             remote(piece, piece, relay_send.at[k, u], j_recv.at[peer, u], partner)
 
+    def asking(k):
+        return pltpu.make_async_remote_copy(
+            src_ref=ask_ref, dst_ref=asks.at[width - k - 1], send_sem=a_send.at[k - 1],
+            recv_sem=a_recv.at[width - k - 1], device_id={"pairs": beside(k)},
+            device_id_type=MESH,
+        )
+
     order = [flags_unit] + list(range(units))
-    for t in range(len(order) + depth + 2):
+    for k in range(1, width):
+        asking(k).start()
+    for t in range(len(order) + depth + 3):
         if t < len(order):
-            for way in (2, 0, 1, 3):
+            for way in range(2):
                 forward(None, p, order[t], way, is_own=True)
         for d in range(1, depth):
             if 0 <= t - d < len(order):
                 gather_z(order[t - d], d)
-        if 0 <= t - depth < len(order):
-            gather_x(order[t - depth])
-            share(order[t - depth])
+        if t == depth - 1:
+            for k in range(1, width):
+                asking(width - k).wait_recv()
+        if 0 <= t - depth + 1 < len(order):
+            offer(order[t - depth + 1])
+        if 0 <= t - depth - 1 < len(order):
+            share(order[t - depth - 1])
         if 1 <= t - depth - 2 < len(order):
             relay(order[t - depth - 2])
 
+    for k in range(1, width):
+        asking(k).wait_send()
+        for u in range(units + 1):
+            crossing(k, u).wait_send()
     for u in range(units):
         c, span = place(u)
         for k in range(hours // CORES):
@@ -321,13 +364,15 @@
 SPLIT = 2
 
 
-def exchange(pair_blocks, whitened, marks, pairs, width, hours):
+def exchange(pair_blocks, asks, whitened, marks, pairs, width, hours):
     rows, cols = whitened.shape[1:]
     part = rows // hours
     units = CHUNKS * SPLIT
     any_space = pl.BlockSpec(memory_space=pl.ANY)
     dma = pltpu.SemaphoreType.DMA
     groups = hours // CORES
+    depth = pairs // width
+    slots = depth + 2 * (width - 1)
     return pl.pallas_call(
         functools.partial(exchange_kernel, pairs, width, hours),
         out_shape=(
@@ -335,15 +380,18 @@
             jax.ShapeDtypeStruct((hours, CHUNKS, part, cols), jnp.bfloat16),
             jax.ShapeDtypeStruct((hours, 2) + marks.shape, jnp.bfloat16),
         ),
-        in_specs=[pl.BlockSpec(memory_space=pltpu.SMEM), any_space, any_space],
+        in_specs=[pl.BlockSpec(memory_space=pltpu.SMEM), any_space, any_space, any_space],
         out_specs=(any_space, any_space, any_space),
-        scratch_shapes=[pltpu.VMEM((pairs, rows // SPLIT, cols), jnp.bfloat16)] * units + [
-            pltpu.VMEM((pairs,) + marks.shape, jnp.bfloat16),
+        scratch_shapes=[pltpu.VMEM((slots, rows // SPLIT, cols), jnp.bfloat16)] * units + [
+            pltpu.VMEM((slots,) + marks.shape, jnp.bfloat16),
             pltpu.VMEM((units, rows // SPLIT, cols), jnp.bfloat16),
             pltpu.VMEM((units, rows // SPLIT, cols), jnp.bfloat16),
             pltpu.VMEM((2,) + marks.shape, jnp.bfloat16),
-            dma((4, pairs, units + 1)),
-            dma((pairs, units + 1)),
+            pltpu.VMEM((width - 1, units, 2, rows // SPLIT, cols), jnp.bfloat16),
+            pltpu.VMEM((width - 1, 2) + marks.shape, jnp.bfloat16),
+            pltpu.VMEM((width - 1,) + asks.shape, asks.dtype),
+            dma((2, depth, units + 1)),
+            dma((depth, units + 1)),
             dma((groups, units)),
             dma((hours, units)),
             dma((groups, units)),
@@ -353,12 +401,16 @@
             dma((hours,)),
             dma((2 * units + 2,)),
             dma((CHUNKS,)),
+            dma((width - 1,)),
+            dma((width - 1,)),
+            dma((width - 1, units + 1)),
+            dma((width - 1, units + 1)),
         ],
         compiler_params=pltpu.CompilerParams(
             collective_id=0, has_side_effects=True, vmem_limit_bytes=32 << 20
         ),
         name="exchange",
-    )(pair_blocks, whitened, marks)
+    )(pair_blocks, asks, whitened, marks)
 
 
 GROUP = 8
@@ -391,12 +443,11 @@
         for c in range(CHUNKS):
             ar = af[h, c, at_rows, :CHUNK]
             ai = af[h, c, at_rows, CHUNK:]
-            for k, value in enumerate((ar, ar + ai, ai - ar)):
+            for k, value in enumerate((ar, ai)):
                 for a in range(GROUP):
-                    heads[a, c, h, k] = jnp.broadcast_to(value[a : a + 1], (8, CHUNK))
-
-    def wide(value):
-        return jnp.concatenate([value] * (BLOCK // 8), axis=0)
+                    heads[a, c, h, k] = jnp.broadcast_to(
+                        value[a : a + 1], (BLOCK, CHUNK)
+                    ).astype(jnp.bfloat16)
 
     for sub in range(GROUP // SUB):
         buf = cross[sub]
@@ -406,20 +457,24 @@
             for r in range(0, rows, BLOCK):
                 tails = []
                 for h in range(hours):
-                    br = bj_ref[h, c, r : r + BLOCK, :CHUNK].astype(f32)
-                    bm = bj_ref[h, c, r : r + BLOCK, CHUNK:].astype(f32)
-                    tails.append((br - bm, bm, br))
+                    tails.append(
+                        (
+                            bj_ref[h, c, r : r + BLOCK, :CHUNK],
+                            bj_ref[h, c, r : r + BLOCK, CHUNK:],
+                        )
+                    )
                 for a in range(SUB):
-                    sums = [None, None, None]
+                    real = imag = None
                     for h in range(hours):
-                        for k in range(3):
-                            term = wide(heads[sub * SUB + a, c, h, k]) * tails[h][k]
-                            sums[k] = term if sums[k] is None else sums[k] + term
+                        ar, ai = heads[sub * SUB + a, c, h, 0], heads[sub * SUB + a, c, h, 1]
+                        br, bm = tails[h]
+                        re = ar * br + ai * bm
+                        im = ai * br - ar * bm
+                        real = re if real is None else real + re
+                        imag = im if imag is None else imag + im
                     at = a * rows + r
-                    buf[at : at + BLOCK, lo:hi] = (sums[0] + sums[1]).astype(jnp.bfloat16)
-                    buf[at : at + BLOCK, hi : hi + CHUNK] = (sums[0] + sums[2]).astype(
-                        jnp.bfloat16
-                    )
+                    buf[at : at + BLOCK, lo:hi] = real
+                    buf[at : at + BLOCK, hi : hi + CHUNK] = imag
         lagged = jnp.dot(buf[...], g_ref[...], preferred_element_type=f32)
         for a in range(SUB):
             k = sub * SUB + a
@@ -439,7 +494,7 @@
             out_specs=pl.BlockSpec((1, GROUP, rows, LAGS), lambda i, *_: (0, i, 0, 0)),
             scratch_shapes=[
                 pltpu.VMEM((hours, CHUNKS, first_rows, cols), jnp.float32),
-                pltpu.VMEM((GROUP, CHUNKS, hours, 3, 8, CHUNK), jnp.float32),
+                pltpu.VMEM((GROUP, CHUNKS, hours, 2, BLOCK, CHUNK), jnp.bfloat16),
                 pltpu.VMEM((rows, rows), jnp.float32),
             ]
             + [pltpu.VMEM((SUB * rows, 2 * F), jnp.bfloat16)] * (GROUP // SUB),
@@ -467,7 +522,7 @@
         out_specs=(vmem, vmem),
         scratch_shapes=[pltpu.VMEM(t.shape, t.dtype) for t in tables]
         + [pltpu.SemaphoreType.DMA((3,))],
-        compiler_params=pltpu.CompilerParams(vmem_limit_bytes=48 << 20),
+        compiler_params=pltpu.CompilerParams(vmem_limit_bytes=63 << 20),
         name="whiten",
     )(samples, usable.reshape(1, rows), *tables)
 
@@ -478,7 +533,10 @@
 
     def body(records, usable, pair_blocks):
         whitened, marks = whiten(records, usable)
-        bj, bi, bf = exchange(pair_blocks, whitened, marks, pairs, width, hours)
+        asks = jnp.broadcast_to(
+            pair_blocks.reshape(2, 1, 1).astype(jnp.float32), (2, 8, 128)
+        )
+        bj, bi, bf = exchange(pair_blocks, asks, whitened, marks, pairs, width, hours)
         me = lax.axis_index("hours").astype(jnp.int32).reshape(1)
         return stack(me, bi, bj, bf, jnp.asarray(lag_weights()))
 

time: 65.7 us -> 61.6 us (0.938)
  local copies, waits for them, and re-layouts: 4.55 us -> 1.71 us
  Pallas kernels: 60.9 us -> 59 us
  other arithmetic: 0 us -> 0.66 us
    pallas_call x1, Pallas kernels: 44.7 us -> 41.3 us  [exchange(): pl.pallas_call(functools.partial(exchange_kernel, pairs, width, hours), o...]
    unnamed x12 -> x8, local copies, waits for them, and re-layouts: 4.55 us -> 1.64 us
    pallas_call x1, Pallas kernels: 4.16 us -> 6.94 us  [whiten(): pl.pallas_call(whiten_kernel, out_shape=(jax.ShapeDtypeStruct((CHUNKS, ro...]
    pallas_call x1, Pallas kernels: 12.1 us -> 10.7 us  [stack(): pl.pallas_call(functools.partial(stack_kernel, hours), grid_spec=pltpu.Pr...]
where the time goes in v3:
time: 61.6 us; the launch traced here: 61.4 us
  Pallas kernels  59 us (96%)
  local copies, waits for them, and re-layouts  1.71 us (3%)
  other arithmetic  0.66 us (1%)
    pallas_call x1, Pallas kernels, exchange(): pl.pallas_call(functools.partial(exchange_kernel, pairs, width, hours), o...  41.3 us
    pallas_call x1, Pallas kernels, stack(): pl.pallas_call(functools.partial(stack_kernel, hours), grid_spec=pltpu.Pr...  10.7 us
    pallas_call x1, Pallas kernels, whiten(): pl.pallas_call(whiten_kernel, out_shape=(jax.ShapeDtypeStruct((CHUNKS, ro...  6.94 us
    unnamed x8, local copies, waits for them, and re-layouts  1.64 us

profile of v3, /device:TPU:1, one launch (start us, length us, event | category | flops | bytes accessed | tf_op | source)
XLA Modules:
  0.0 61.4 jit_solution(14135182195470029484)
XLA Ops:
  0.0 0.7 %convert_bitcast_fusion = f32[2]{0:T(128)S(1)} fusion(s32[1,2]{1,0:T(1,128)} %pair_ref.1), kind=kLoop, calls=%fused_computation | loop fusion | flops 2 | bytes 16 | tf_op jit(solution)/shard_map/convert_element_type | solution.py:537
  0.7 0.1 broadcast_in_dim.2.ask_ref
  0.7 0.0 copy-start.3
  0.7 0.0 copy-start
  0.7 6.9 %whiten.1 = (bf16[4,128,256]{2,1,0:T(8,128)(2,1)}, bf16[16,128]{1,0:T(8,128)(2,1)}) custom-call(bf16[3600,128]{1,0:T(8,128)(2,1)} %bitcast.7, s32[1,128]{1,0:T(1,128)} %bitcast.8, bf16[576,1800]{1,0:T(8,128)(2,1)} %constant.12.clone.even_hbm, bf16[576,1800]{1,0:T(8,128)(2,1)} %constant.13.clone.odd_hbm, bf16[512,576]{1,0:T(8,128)(2,1)} %constant.14.clone.ones_hbm), custom_call_target="tpu_custom_call" | custom-call | tf_op jit(solution)/shard_map/whiten/pallas_call | solution.py:515
  7.7 0.0 copy-done.3
  7.7 0.0 copy-start.1
  7.7 0.9 %copy-done.1 = bf16[4,128,256]{2,1,0:T(8,128)(2,1)S(1)} copy-done((bf16[4,128,256]{2,1,0:T(8,128)(2,1)S(1)}, bf16[4,128,256]{2,1,0:T(8,128)(2,1)}, u32[]{:S(2)}) %copy-start.1) | copy-done | bytes 262168
  8.7 0.0 copy-start.2
  8.7 0.7 %copy-done.2 = bf16[16,128]{1,0:T(8,128)(2,1)S(1)} copy-done((bf16[16,128]{1,0:T(8,128)(2,1)S(1)}, bf16[16,128]{1,0:T(8,128)(2,1)}, u32[]{:S(2)}) %copy-start.2) | copy-done | bytes 4120
  9.3 41.3 %exchange.1 = (bf16[4,4,128,256]{3,2,1,0:T(8,128)(2,1)S(1)}, bf16[4,4,32,256]{3,2,1,0:T(8,128)(2,1)S(1)}, bf16[4,2,16,128]{3,2,1,0:T(8,128)(2,1)S(1)}) custom-call(s32[1,2]{1,0:T(1,128)S(1)} %copy-done.3, f32[2,8,128]{2,1,0:T(8,128)S(1)} %broadcast_in_dim.2.ask_ref, bf16[4,128,256]{2,1,0:T(8,128)(2,1)S(1)} %copy-done.1, bf16[16,128]{1,0:T(8,128)(2,1)S(1)} %copy-done.2), custom_call_target="tpu_custom_call" | custom-call | tf_op jit(solution)/shard_map/exchange/pallas_call | solution.py:376
  50.7 0.0 copy-done
  50.7 10.7 %stack.1 = f32[1,32,128,256]{3,2,1,0:T(8,128)} custom-call(s32[1]{0:T(128)} %bitcast.me_ref, bf16[4,4,32,256]{3,2,1,0:T(8,128)(2,1)S(1)} %get-tuple-element.12.bi_ref, bf16[4,4,128,256]{3,2,1,0:T(8,128)(2,1)S(1)} %get-tuple-element.13.bj_ref, bf16[4,2,16,128]{3,2,1,0:T(8,128)(2,1)S(1)} %get-tuple-element.14.bf_ref, bf16[1024,256]{1,0:T(8,128)(2,1)S(1)} %copy-done), custom_call_target="tpu_custom_call" | custom-call | tf_op jit(solution)/shard_map/stack/pallas_call | solution.py:488
Async XLA Ops:
  0.7 7.0 %copy-start.3 = (s32[1,2]{1,0:T(1,128)S(1)}, s32[1,2]{1,0:T(1,128)}, u32[]{:S(2)}) copy-start(s32[1,2]{1,0:T(1,128)} %pair_ref.1) | copy-start | bytes 28
  0.7 49.9 %copy-start = (bf16[1024,256]{1,0:T(8,128)(2,1)S(1)}, bf16[1024,256]{1,0:T(8,128)(2,1)}, u32[]{:S(2)}) copy-start(bf16[1024,256]{1,0:T(8,128)(2,1)} %constant.15.clone.g_ref) | copy-start | bytes 1572868
  7.7 1.0 %copy-start.1 = (bf16[4,128,256]{2,1,0:T(8,128)(2,1)S(1)}, bf16[4,128,256]{2,1,0:T(8,128)(2,1)}, u32[]{:S(2)}) copy-start(bf16[4,128,256]{2,1,0:T(8,128)(2,1)} %get-tuple-element.10.w_ref) | copy-start | bytes 786436
  8.7 0.7 %copy-start.2 = (bf16[16,128]{1,0:T(8,128)(2,1)S(1)}, bf16[16,128]{1,0:T(8,128)(2,1)}, u32[]{:S(2)}) copy-start(bf16[16,128]{1,0:T(8,128)(2,1)} %get-tuple-element.11.f_ref) | copy-start | bytes 12292
